TPU v7x, 256 devices: a whole 4x4x8 slice. The times are simulated.
256 devices in a mesh: row: 16 (over x, z_hi, core), col: 16 (over z_lo, y).
Axes of the slice: x: 4, y: 4, z: 8 (z_hi: 2, z_lo: 4; z = z_hi * 4 + z_lo), core: 2. Of those that a mesh axis runs over, the one named last changes fastest.
Arguments:
- ancestor_inverse: bfloat16 [24576, 24576], P('row', 'col'), may hold values from -0.0390625 to 0.0390625
- panels: bfloat16 [24576, 3, 512], P(('row', 'col')), may hold values from -1.1953125 to 1.1953125
- diag_inverse: float32 [3, 512, 512], replicated, may hold values from -6 to 6
- tile_mask: int32 [3, 192], replicated, may hold values 0 or 1
Outputs:
- off_diagonal: float32 [24576, 3, 512], P(('row', 'col'))
- diagonal: float32 [3, 512, 512], replicated
All inputs are finite; a program needn't handle non-finite values.
Results may differ from a plain program's by a relative error of at most 0.0003.
Values may be sent and summed in bfloat16 or wider, within the bound.
No kernel may reach another device: no remote copies, remote signals or barrier semaphores. Data moves between devices by JAX's collectives and lax.ppermute only.
A program may use at most 192 MiB of HBM per device.

v0:
```python
import jax
import jax.numpy as jnp
from jax import lax
from jax.sharding import PartitionSpec as P

TILE = 128
ALL = ("row", "col")


def body(ancestor_inverse, panels, diag_inverse, tile_mask):
    rows, cols = (lax.axis_size("row"), lax.axis_size("col"))
    row_index, col_index = (lax.axis_index("row"), lax.axis_index("col"))
    kept, count, width = panels.shape
    start = (row_index * cols + col_index) * kept
    tile_of = (start + jnp.arange(kept)) // TILE
    own_mask = jnp.take(tile_mask, tile_of, axis=1).astype(jnp.bfloat16)
    masked = jnp.swapaxes(panels, 0, 1) * own_mask[:, :, None]
    flip = [(i * cols + j, j * cols + i) for i in range(rows) for j in range(cols)]
    turned = lax.ppermute(masked, ALL, flip)
    blocks = []
    for p in range(count):
        gathered = lax.all_gather(turned[p], "row", axis=0, tiled=True)
        partial = jnp.dot(ancestor_inverse, gathered, preferred_element_type=jnp.float32)
        summed = lax.psum_scatter(partial, "col", scatter_dimension=0, tiled=True)
        blocks.append(-summed)
    off_diagonal = jnp.stack(blocks)
    schur = jnp.einsum(
        "pma,pmb->pab", masked.astype(jnp.float32), off_diagonal, precision=lax.Precision.HIGHEST
    )
    lines = schur.reshape(count * width, width)
    share = lax.psum_scatter(lines, "col", scatter_dimension=0, tiled=True)
    share = lax.psum(share, "row")
    total = lax.all_gather(share, "col", axis=0, tiled=True)
    return (jnp.swapaxes(off_diagonal, 0, 1), diag_inverse - total.reshape(schur.shape))


def solution(mesh):
    placed = (P("row", "col"), P(ALL, None, None), P(), P())
    return jax.shard_map(
        body, mesh=mesh, in_specs=placed, out_specs=(P(ALL, None, None), P()), check_vma=False
    )
```

profile of v0, /device:TPU:2, one launch (start us, length us, event | category | flops | bytes accessed | tf_op | source)
XLA Modules:
  0.0 855.5 jit_solution(13379166648206793179)
XLA Ops:
  7.2 0.0 all-gather.14.cloned.1.call-start
  7.3 0.8 copy.10
  8.1 0.6 gather_fusion
  8.7 0.1 fusion.5
  8.8 0.1 copy.11
  8.9 1.1 bitcast_multiply_fusion
  10.0 3.8 collective-permute-start
  13.8 32.1 %collective-permute-done = bf16[3,96,512]{2,1,0:T(8,128)(2,1)S(1)} collective-permute-done((bf16[3,96,512]{2,1,0:T(8,128)(2,1)S(1)}, bf16[3,96,512]{2,1,0:T(8,128)(2,1)S(1)}, u32[]{:S(2)}, u32[]{:S(2)}) %collective-permute-start) | collective-permute-done | bytes 294944 | tf_op jit(solution)/shard_map/ppermute | solution.py:19
  45.8 0.7 fusion.8
  46.5 0.0 all-gather.14.cloned.1.call-update
  46.6 0.0 all-gather.12.cloned.1.call-start
  46.6 0.7 all-gather.12.cloned.1.call-update
  47.3 0.0 all-gather.10.cloned.1.call-start
  47.4 0.7 all-gather.10.cloned.1.call-update
  48.1 0.0 reduce-scatter.17.cloned.1.call-start
  48.1 61.7 %all-gather.14.cloned.1.call-done = bf16[1,1536,512]{2,1,0:T(8,128)(2,1)} async-done(((bf16[1,96,512]{2,1,0:T(8,128)(2,1)}), bf16[1,1536,512]{2,1,0:T(8,128)(2,1)}) %all-gather.14.cloned.1.call-update) | async-done | bytes 1572880 | tf_op jit(solution)/shard_map/all_gather | solution.py:22
  109.8 5.0 convolution_bitcast_fusion
  114.8 2.4 copy.19
  117.2 0.0 reduce-scatter.17.cloned.1.call-update
  117.2 0.0 reduce-scatter.15.cloned.1.call-start
  117.3 50.4 %all-gather.12.cloned.1.call-done = bf16[1,1536,512]{2,1,0:T(8,128)(2,1)} async-done(((bf16[1,96,512]{2,1,0:T(8,128)(2,1)}), bf16[1,1536,512]{2,1,0:T(8,128)(2,1)}) %all-gather.12.cloned.1.call-update) | async-done | bytes 1572880 | tf_op jit(solution)/shard_map/all_gather | solution.py:22
  167.7 5.0 convolution_bitcast_fusion.1
  172.7 2.4 copy.17
  175.1 0.0 reduce-scatter.15.cloned.1.call-update
  175.1 0.0 reduce-scatter.13.cloned.1.call-start
  175.1 51.0 %all-gather.10.cloned.1.call-done = bf16[1,1536,512]{2,1,0:T(8,128)(2,1)} async-done(((bf16[1,96,512]{2,1,0:T(8,128)(2,1)}), bf16[1,1536,512]{2,1,0:T(8,128)(2,1)}) %all-gather.10.cloned.1.call-update) | async-done | bytes 1572880 | tf_op jit(solution)/shard_map/all_gather | solution.py:22
  226.1 5.0 convolution_bitcast_fusion.2
  231.2 2.4 copy.15
  233.6 0.0 reduce-scatter.13.cloned.1.call-update
  233.6 0.0 reduce-scatter.11.cloned.1.call-start
  233.6 83.0 %reduce-scatter.17.cloned.1.call-done = f32[96,512]{1,0:T(8,128)} async-done(((f32[1536,512]{1,0:T(8,128)}), f32[96,512]{1,0:T(8,128)}) %reduce-scatter.17.cloned.1.call-update) | async-done | bytes 196624 | tf_op jit(solution)/shard_map/reduce_scatter | solution.py:24
  316.6 0.9 negate_bitcast_fusion
  317.5 89.1 %reduce-scatter.15.cloned.1.call-done = f32[96,512]{1,0:T(8,128)} async-done(((f32[1536,512]{1,0:T(8,128)}), f32[96,512]{1,0:T(8,128)}) %reduce-scatter.15.cloned.1.call-update) | async-done | bytes 196624 | tf_op jit(solution)/shard_map/reduce_scatter | solution.py:24
  406.6 0.9 negate_bitcast_fusion.1
  407.6 89.0 %reduce-scatter.13.cloned.1.call-done = f32[96,512]{1,0:T(8,128)} async-done(((f32[1536,512]{1,0:T(8,128)}), f32[96,512]{1,0:T(8,128)}) %reduce-scatter.13.cloned.1.call-update) | async-done | bytes 196624 | tf_op jit(solution)/shard_map/reduce_scatter | solution.py:24
  496.6 0.9 negate_bitcast_fusion.2
  497.5 0.0 copy-start.1
  497.5 0.7 copy-done.1
  498.2 3.1 fusion.3
  501.3 0.0 copy-start
  501.3 0.0 reduce-scatter.11.cloned.1.call-update
  501.3 0.0 all-reduce.2.cloned.1.call-start
  501.4 87.6 %reduce-scatter.11.cloned.1.call-done = f32[96,512]{1,0:T(8,128)} async-done(((f32[1536,512]{1,0:T(8,128)}), f32[96,512]{1,0:T(8,128)}) %reduce-scatter.11.cloned.1.call-update) | async-done | bytes 196624 | tf_op jit(solution)/shard_map/reduce_scatter | solution.py:31
  589.0 0.0 all-reduce.2.cloned.1.call-update
  589.0 0.0 all-gather.8.cloned.1.call-start
  589.1 163.7 %all-reduce.2.cloned.1.call-done = f32[96,512]{1,0:T(8,128)} async-done(((f32[96,512]{1,0:T(8,128)}), f32[96,512]{1,0:T(8,128)}) %all-reduce.2.cloned.1.call-update) | async-done | bytes 196624 | tf_op jit(solution)/shard_map/psum | solution.py:32
  752.8 0.0 all-gather.8.cloned.1.call-update
  752.9 1.8 fusion.4
  754.6 90.0 %all-gather.8.cloned.1.call-done = f32[1536,512]{1,0:T(8,128)} async-done(((f32[96,512]{1,0:T(8,128)}), f32[1536,512]{1,0:T(8,128)}) %all-gather.8.cloned.1.call-update) | async-done | bytes 3145744 | tf_op jit(solution)/shard_map/all_gather | solution.py:33
  844.7 0.0 copy-done
  844.7 4.3 sub.13
  (3 shorter events, 0.0 us)
Async XLA Ops:
  7.2 102.6 %all-gather.14.cloned.1.call-start = ((), (), s32[]{:S(2)}) async-start(), calls=%async_computation.9 | async-start | bytes 1671168 | tf_op jit(solution)/shard_map/all_gather | solution.py:22
  10.0 35.9 %collective-permute-start = (bf16[3,96,512]{2,1,0:T(8,128)(2,1)S(1)}, bf16[3,96,512]{2,1,0:T(8,128)(2,1)S(1)}, u32[]{:S(2)}, u32[]{:S(2)}) collective-permute-start(bf16[3,96,512]{2,1,0:T(8,128)(2,1)S(1)} %bitcast_multiply_fusion), channel_id=1, source_target_pairs={{0,0},{1,16},{2,32},{3,48},{4,64},{5,80},{6,96},{7,112},{8,128},{9... | collective-permute-start | bytes 884744 | tf_op jit(solution)/shard_map/ppermute | solution.py:19
  46.6 121.1 %all-gather.12.cloned.1.call-start = ((), (), s32[]{:S(2)}) async-start(), calls=%async_computation.8 | async-start | bytes 1671168 | tf_op jit(solution)/shard_map/all_gather | solution.py:22
  47.3 178.8 %all-gather.10.cloned.1.call-start = ((), (), s32[]{:S(2)}) async-start(), calls=%async_computation.7 | async-start | bytes 1671168 | tf_op jit(solution)/shard_map/all_gather | solution.py:22
  48.1 268.5 %reduce-scatter.17.cloned.1.call-start = ((), (), s32[]{:S(2)}) async-start(), calls=%async_computation.12 | async-start | bytes 3342336 | tf_op jit(solution)/shard_map/reduce_scatter | solution.py:24
  117.2 289.4 %reduce-scatter.15.cloned.1.call-start = ((), (), s32[]{:S(2)}) async-start(), calls=%async_computation.11 | async-start | bytes 3342336 | tf_op jit(solution)/shard_map/reduce_scatter | solution.py:24
  175.1 321.5 %reduce-scatter.13.cloned.1.call-start = ((), (), s32[]{:S(2)}) async-start(), calls=%async_computation.10 | async-start | bytes 3342336 | tf_op jit(solution)/shard_map/reduce_scatter | solution.py:24
  233.6 355.4 %reduce-scatter.11.cloned.1.call-start = ((), (), s32[]{:S(2)}) async-start(), calls=%async_computation.4 | async-start | bytes 3342336 | tf_op jit(solution)/shard_map/reduce_scatter | solution.py:31
  497.5 0.7 copy-start.1
  501.3 343.4 %copy-start = (f32[3,512,512]{2,1,0:T(8,128)S(1)}, f32[3,512,512]{2,1,0:T(8,128)}, u32[]{:S(2)}) copy-start(f32[3,512,512]{2,1,0:T(8,128)} %param.6) | copy-start | bytes 9437188
  501.3 251.5 %all-reduce.2.cloned.1.call-start = ((), (), s32[]{:S(2)}) async-start(), calls=%async_computation.5 | async-start | bytes 393216 | tf_op jit(solution)/shard_map/psum | solution.py:32
  589.0 255.6 %all-gather.8.cloned.1.call-start = ((), (), s32[]{:S(2)}) async-start(), calls=%async_computation.6 | async-start | bytes 3342336 | tf_op jit(solution)/shard_map/all_gather | solution.py:33
Sparse Core Ops, SparseCore 0:
  46.7 63.0 all-gather.13
  112.5 55.1 all-gather.11
  170.9 55.1 all-gather.9
  229.1 87.4 reduce-scatter.16
  319.0 87.5 reduce-scatter.14
  409.0 87.5 reduce-scatter.12
  501.5 87.5 reduce-scatter.10
  591.6 161.1 all-reduce.1
  754.8 89.8 all-gather.7
where the time goes:
time: 856 us
  waiting for transfers between devices  799 us (93%)
  matrix products  18.1 us (2%)
  between operations  13.9 us (2%)
  other arithmetic  10.1 us (1%)
  local copies, waits for them, and re-layouts  10 us (1%)
    reduce_scatter x3, waiting for transfers between devices, body(): summed = lax.psum_scatter(partial, 'col', scatter_dimension=0, tiled=True)  261 us
    psum x1, waiting for transfers between devices, body(): share = lax.psum(share, 'row')  164 us
    all_gather x3, waiting for transfers between devices, body(): gathered = lax.all_gather(turned[p], 'row', axis=0, tiled=True)  163 us
    all_gather x1, waiting for transfers between devices, body(): total = lax.all_gather(share, 'col', axis=0, tiled=True)  90 us
    reduce_scatter x1, waiting for transfers between devices, body(): share = lax.psum_scatter(lines, 'col', scatter_dimension=0, tiled=True)  87.6 us
    ppermute x1, waiting for transfers between devices, body(): turned = lax.ppermute(masked, ALL, flip)  32.1 us
  transfers between devices with their start and end apart: 10, of which 10 were waited for; matrix products, arithmetic and copies ran while one was open for 3% of the time, Pallas kernels for 0%

commit v1 on v0

--- a/solution.py
+++ b/solution.py
@@ -29,7 +29,7 @@
     )
     lines = schur.reshape(count * width, width)
     share = lax.psum_scatter(lines, "col", scatter_dimension=0, tiled=True)
-    share = lax.psum(share, "row")
+    share = jnp.sum(lax.all_gather(share, "row"), axis=0)
     total = lax.all_gather(share, "col", axis=0, tiled=True)
     return (jnp.swapaxes(off_diagonal, 0, 1), diag_inverse - total.reshape(schur.shape))
 

time: 856 us -> 754 us (0.88)
  waiting for transfers between devices: 799 us -> 695 us
    psum x1 -> x0, waiting for transfers between devices: 164 us -> none  [body(): share = lax.psum(share, 'row')]
    all_gather x0 -> x1, waiting for transfers between devices: none -> 68.8 us  [body(): share = jnp.sum(lax.all_gather(share, 'row'), axis=0)]
    all_gather x1, waiting for transfers between devices: 90 us -> 80.4 us  [body(): total = lax.all_gather(share, 'col', axis=0, tiled=True)]
where the time goes in v1:
time: 754 us
  waiting for transfers between devices  695 us (92%)
  matrix products  18.1 us (2%)
  between operations  14 us (2%)
  other arithmetic  13 us (2%)
  local copies, waits for them, and re-layouts  10 us (1%)
    reduce_scatter x3, waiting for transfers between devices, body(): summed = lax.psum_scatter(partial, 'col', scatter_dimension=0, tiled=True)  261 us
    all_gather x3, waiting for transfers between devices, body(): gathered = lax.all_gather(turned[p], 'row', axis=0, tiled=True)  163 us
    reduce_scatter x1, waiting for transfers between devices, body(): share = lax.psum_scatter(lines, 'col', scatter_dimension=0, tiled=True)  87.6 us
    all_gather x1, waiting for transfers between devices, body(): total = lax.all_gather(share, 'col', axis=0, tiled=True)  80.4 us
    all_gather x1, waiting for transfers between devices, body(): share = jnp.sum(lax.all_gather(share, 'row'), axis=0)  68.8 us
    ppermute x1, waiting for transfers between devices, body(): turned = lax.ppermute(masked, ALL, flip)  32.1 us
  transfers between devices with their start and end apart: 10, of which 10 were waited for; matrix products, arithmetic and copies ran while one was open for 3% of the time, Pallas kernels for 0%

profile of v1, /device:TPU:2, one launch (start us, length us, event | category | flops | bytes accessed | tf_op | source)
XLA Modules:
  0.0 753.8 jit_solution(11475509827075779442)
XLA Ops:
  7.2 0.0 all-gather.16.cloned.1.call-start
  7.3 0.8 copy.10
  8.1 0.6 gather_fusion
  8.7 0.1 fusion.5
  8.8 0.1 copy.11
  8.9 1.1 bitcast_multiply_fusion
  10.0 3.8 collective-permute-start
  13.8 32.1 %collective-permute-done = bf16[3,96,512]{2,1,0:T(8,128)(2,1)S(1)} collective-permute-done((bf16[3,96,512]{2,1,0:T(8,128)(2,1)S(1)}, bf16[3,96,512]{2,1,0:T(8,128)(2,1)S(1)}, u32[]{:S(2)}, u32[]{:S(2)}) %collective-permute-start) | collective-permute-done | bytes 294944 | tf_op jit(solution)/shard_map/ppermute | solution.py:19
  45.8 0.7 fusion.8
  46.5 0.0 all-gather.16.cloned.1.call-update
  46.6 0.0 all-gather.14.cloned.1.call-start
  46.6 0.7 all-gather.14.cloned.1.call-update
  47.3 0.0 all-gather.12.cloned.1.call-start
  47.4 0.7 all-gather.12.cloned.1.call-update
  48.1 0.0 reduce-scatter.17.cloned.1.call-start
  48.1 61.7 %all-gather.16.cloned.1.call-done = bf16[1,1536,512]{2,1,0:T(8,128)(2,1)} async-done(((bf16[1,96,512]{2,1,0:T(8,128)(2,1)}), bf16[1,1536,512]{2,1,0:T(8,128)(2,1)}) %all-gather.16.cloned.1.call-update) | async-done | bytes 1572880 | tf_op jit(solution)/shard_map/all_gather | solution.py:22
  109.8 5.0 convolution_bitcast_fusion
  114.8 2.4 copy.19
  117.2 0.0 reduce-scatter.17.cloned.1.call-update
  117.2 0.0 reduce-scatter.15.cloned.1.call-start
  117.3 50.4 %all-gather.14.cloned.1.call-done = bf16[1,1536,512]{2,1,0:T(8,128)(2,1)} async-done(((bf16[1,96,512]{2,1,0:T(8,128)(2,1)}), bf16[1,1536,512]{2,1,0:T(8,128)(2,1)}) %all-gather.14.cloned.1.call-update) | async-done | bytes 1572880 | tf_op jit(solution)/shard_map/all_gather | solution.py:22
  167.7 5.0 convolution_bitcast_fusion.1
  172.7 2.4 copy.17
  175.1 0.0 reduce-scatter.15.cloned.1.call-update
  175.1 0.0 reduce-scatter.13.cloned.1.call-start
  175.1 51.0 %all-gather.12.cloned.1.call-done = bf16[1,1536,512]{2,1,0:T(8,128)(2,1)} async-done(((bf16[1,96,512]{2,1,0:T(8,128)(2,1)}), bf16[1,1536,512]{2,1,0:T(8,128)(2,1)}) %all-gather.12.cloned.1.call-update) | async-done | bytes 1572880 | tf_op jit(solution)/shard_map/all_gather | solution.py:22
  226.1 5.0 convolution_bitcast_fusion.2
  231.2 2.4 copy.15
  233.6 0.0 reduce-scatter.13.cloned.1.call-update
  233.6 0.0 reduce-scatter.11.cloned.1.call-start
  233.6 83.0 %reduce-scatter.17.cloned.1.call-done = f32[96,512]{1,0:T(8,128)} async-done(((f32[1536,512]{1,0:T(8,128)}), f32[96,512]{1,0:T(8,128)}) %reduce-scatter.17.cloned.1.call-update) | async-done | bytes 196624 | tf_op jit(solution)/shard_map/reduce_scatter | solution.py:24
  316.6 0.9 negate_bitcast_fusion
  317.5 89.1 %reduce-scatter.15.cloned.1.call-done = f32[96,512]{1,0:T(8,128)} async-done(((f32[1536,512]{1,0:T(8,128)}), f32[96,512]{1,0:T(8,128)}) %reduce-scatter.15.cloned.1.call-update) | async-done | bytes 196624 | tf_op jit(solution)/shard_map/reduce_scatter | solution.py:24
  406.6 0.9 negate_bitcast_fusion.1
  407.6 89.0 %reduce-scatter.13.cloned.1.call-done = f32[96,512]{1,0:T(8,128)} async-done(((f32[1536,512]{1,0:T(8,128)}), f32[96,512]{1,0:T(8,128)}) %reduce-scatter.13.cloned.1.call-update) | async-done | bytes 196624 | tf_op jit(solution)/shard_map/reduce_scatter | solution.py:24
  496.6 0.9 negate_bitcast_fusion.2
  497.5 0.0 copy-start.1
  497.5 0.7 copy-done.1
  498.2 3.1 fusion.3
  501.3 0.0 reduce-scatter.11.cloned.1.call-update
  501.3 0.0 copy-start
  501.4 0.0 all-gather.18.cloned.1.call-start
  501.4 87.6 %reduce-scatter.11.cloned.1.call-done = f32[96,512]{1,0:T(8,128)} async-done(((f32[1536,512]{1,0:T(8,128)}), f32[96,512]{1,0:T(8,128)}) %reduce-scatter.11.cloned.1.call-update) | async-done | bytes 196624 | tf_op jit(solution)/shard_map/reduce_scatter | solution.py:31
  589.0 0.0 all-gather.18.cloned.1.call-update
  589.0 0.0 all-gather.10.cloned.1.call-start
  589.1 68.8 %all-gather.18.cloned.1.call-done = f32[1536,512]{1,0:T(8,128)} async-done(((f32[96,512]{1,0:T(8,128)}), f32[1536,512]{1,0:T(8,128)}) %all-gather.18.cloned.1.call-update) | async-done | bytes 3145744 | tf_op jit(solution)/shard_map/all_gather | solution.py:32
  657.9 2.9 reduce_sum.9
  660.8 0.0 all-gather.10.cloned.1.call-update
  660.8 1.8 fusion.4
  662.6 80.4 %all-gather.10.cloned.1.call-done = f32[1536,512]{1,0:T(8,128)} async-done(((f32[96,512]{1,0:T(8,128)}), f32[1536,512]{1,0:T(8,128)}) %all-gather.10.cloned.1.call-update) | async-done | bytes 3145744 | tf_op jit(solution)/shard_map/all_gather | solution.py:33
  743.0 0.0 copy-done
  743.0 4.3 sub.13
  (3 shorter events, 0.0 us)
Async XLA Ops:
  7.2 102.6 %all-gather.16.cloned.1.call-start = ((), (), s32[]{:S(2)}) async-start(), calls=%async_computation.8 | async-start | bytes 1671168 | tf_op jit(solution)/shard_map/all_gather | solution.py:22
  10.0 35.9 %collective-permute-start = (bf16[3,96,512]{2,1,0:T(8,128)(2,1)S(1)}, bf16[3,96,512]{2,1,0:T(8,128)(2,1)S(1)}, u32[]{:S(2)}, u32[]{:S(2)}) collective-permute-start(bf16[3,96,512]{2,1,0:T(8,128)(2,1)S(1)} %bitcast_multiply_fusion), channel_id=1, source_target_pairs={{0,0},{1,16},{2,32},{3,48},{4,64},{5,80},{6,96},{7,112},{8,128},{9... | collective-permute-start | bytes 884744 | tf_op jit(solution)/shard_map/ppermute | solution.py:19
  46.6 121.1 %all-gather.14.cloned.1.call-start = ((), (), s32[]{:S(2)}) async-start(), calls=%async_computation.7 | async-start | bytes 1671168 | tf_op jit(solution)/shard_map/all_gather | solution.py:22
  47.3 178.8 %all-gather.12.cloned.1.call-start = ((), (), s32[]{:S(2)}) async-start(), calls=%async_computation.6 | async-start | bytes 1671168 | tf_op jit(solution)/shard_map/all_gather | solution.py:22
  48.1 268.5 %reduce-scatter.17.cloned.1.call-start = ((), (), s32[]{:S(2)}) async-start(), calls=%async_computation.12 | async-start | bytes 3342336 | tf_op jit(solution)/shard_map/reduce_scatter | solution.py:24
  117.2 289.4 %reduce-scatter.15.cloned.1.call-start = ((), (), s32[]{:S(2)}) async-start(), calls=%async_computation.11 | async-start | bytes 3342336 | tf_op jit(solution)/shard_map/reduce_scatter | solution.py:24
  175.1 321.5 %reduce-scatter.13.cloned.1.call-start = ((), (), s32[]{:S(2)}) async-start(), calls=%async_computation.10 | async-start | bytes 3342336 | tf_op jit(solution)/shard_map/reduce_scatter | solution.py:24
  233.6 355.4 %reduce-scatter.11.cloned.1.call-start = ((), (), s32[]{:S(2)}) async-start(), calls=%async_computation.4 | async-start | bytes 3342336 | tf_op jit(solution)/shard_map/reduce_scatter | solution.py:31
  497.5 0.7 copy-start.1
  501.3 241.6 %copy-start = (f32[3,512,512]{2,1,0:T(8,128)S(1)}, f32[3,512,512]{2,1,0:T(8,128)}, u32[]{:S(2)}) copy-start(f32[3,512,512]{2,1,0:T(8,128)} %param.6) | copy-start | bytes 9437188
  501.4 156.5 %all-gather.18.cloned.1.call-start = ((), (), s32[]{:S(2)}) async-start(), calls=%async_computation.9 | async-start | bytes 3342336 | tf_op jit(solution)/shard_map/all_gather | solution.py:32
  589.0 153.9 %all-gather.10.cloned.1.call-start = ((), (), s32[]{:S(2)}) async-start(), calls=%async_computation.5 | async-start | bytes 3342336 | tf_op jit(solution)/shard_map/all_gather | solution.py:33
Sparse Core Ops, SparseCore 0:
  46.7 63.0 all-gather.15
  112.5 55.1 all-gather.13
  170.9 55.1 all-gather.11
  229.1 87.4 reduce-scatter.16
  319.0 87.5 reduce-scatter.14
  409.0 87.5 reduce-scatter.12
  501.5 87.5 reduce-scatter.10
  591.7 66.1 all-gather.17
  660.9 82.0 all-gather.9
